TPU v7x, 32 devices: a whole 2x2x4 slice. The times are simulated.
32 devices in a mesh: prow: 8 (over y, x, core), pcol: 4 (over z).
Axes of the slice: x: 2, y: 2, z: 4, core: 2. Of those that a mesh axis runs over, the one named last changes fastest.
Arguments:
- matrix: float32 [4096, 4096], P('prow', 'pcol'), may hold values from -6 to 6
- pivots: int32 [2, 512], replicated, may hold values from 0 to 4095, as said below
- lower_inv: float32 [2, 512, 512], replicated, as said below
- upper_inv: float32 [2, 512, 512], replicated, as said below
Outputs:
- factored: float32 [4096, 4096], P('prow', 'pcol')
Inputs may be any that keep to these rules, and one draw needn't show every extreme that they name: The entries of pivots[k] are distinct row indices from k * 512 to 4095. Each lower_inv[k] is lower triangular. Each upper_inv[k] is upper triangular.
All inputs are finite; a program needn't handle non-finite values.
Results may differ from a plain program's by a relative error of at most 0.0001.
Values sent between devices are 32-bit elements; how exact they have to be, the bound alone decides.
No kernel may reach another device: no remote copies, remote signals or barrier semaphores. Data moves between devices by JAX's collectives and lax.ppermute only.
A program may use at most 128 MiB of HBM per device.

v0:
```python
import jax
import jax.numpy as jnp
from jax import lax
from jax.sharding import PartitionSpec as P


def broadcast(block, axis, holder):
    block = jnp.where(lax.axis_index(axis) == holder, block, jnp.zeros_like(block))
    return lax.psum(block, axis)


def displaced(pivot_row, start_row):
    width = pivot_row.shape[0]
    end_row = start_row + width
    window = start_row + jnp.arange(width, dtype=jnp.int32)
    chosen = jnp.any(pivot_row[None, :] == window[:, None], axis=1)
    unnamed = jnp.logical_not(chosen)
    free_rank = jnp.cumsum(unnamed.astype(jnp.int32)) - 1
    outside = pivot_row >= end_row
    out_rank = jnp.sum(
        (outside[None, :] & (pivot_row[None, :] < pivot_row[:, None])).astype(jnp.int32), axis=1
    )
    matches = unnamed[None, :] & (free_rank[None, :] == out_rank[:, None])
    source = jnp.sum(jnp.where(matches, window[None, :], 0), axis=1)
    return (source, outside)


def product(left, right):
    return jnp.dot(left, right, precision=lax.Precision.HIGHEST, preferred_element_type=jnp.float32)


def shards(matrix, pivots, lower_inv, upper_inv):
    local_rows, local_cols = matrix.shape
    block_width = lower_inv.shape[1]
    first_row = lax.axis_index("prow") * local_rows
    row_ids = first_row + jnp.arange(local_rows, dtype=jnp.int32)
    col_ids = lax.axis_index("pcol") * local_cols + jnp.arange(local_cols, dtype=jnp.int32)
    current = matrix
    for panel_index in range(pivots.shape[0]):
        start_row = panel_index * block_width
        end_row = start_row + block_width
        wanted = pivots[panel_index]
        offset = wanted - first_row
        owned_rows = (offset >= 0) & (offset < local_rows)
        gathered_rows = jnp.take(current, jnp.clip(offset, 0, local_rows - 1), axis=0)
        picked = jnp.where(owned_rows[:, None], gathered_rows, 0.0)
        beyond = col_ids >= end_row
        reduced = lax.psum_scatter(picked, "prow", scatter_dimension=0, tiled=True)
        raw_top = lax.all_gather(reduced, "prow", axis=0, tiled=True)
        solved = product(lower_inv[panel_index], raw_top)
        top_block = jnp.where(beyond[None, :], solved, raw_top)
        top_masked = jnp.where(beyond[None, :], solved, 0.0)
        owner_row = start_row // local_rows
        first_local = start_row - owner_row * local_rows
        local_top = current
        old_top = broadcast(local_top, "prow", owner_row)
        source, outside = displaced(wanted, start_row)
        dest_local = jnp.where(outside & owned_rows, offset, local_rows)
        moved = jnp.take(old_top, jnp.clip(source - start_row, 0, block_width - 1), axis=0)
        swapped = current.at[dest_local].set(moved, mode="drop")
        is_owner = lax.axis_index("prow") == owner_row
        top_slice = swapped
        swapped = swapped.at[first_local : first_local + block_width].set(
            jnp.where(is_owner, top_block, top_slice)
        )
        owner_col = start_row // local_cols
        left_col = start_row - owner_col * local_cols
        column_panel = product(
            swapped[:, left_col : left_col + block_width], upper_inv[panel_index]
        )
        lower_block = broadcast(column_panel, "pcol", owner_col)
        below_rows = row_ids >= end_row
        lower_masked = jnp.where(below_rows[:, None], lower_block, 0.0)
        updated = swapped - product(lower_masked, top_masked)
        panel_slice = updated[:, left_col : left_col + block_width]
        col_owner = lax.axis_index("pcol") == owner_col
        new_panel = jnp.where(below_rows[:, None] & col_owner, lower_block, panel_slice)
        current = updated.at[:, left_col : left_col + block_width].set(new_panel)
    return current


def solution(mesh):
    in_specs = (P("prow", "pcol"), P(), P(), P())
    out_specs = P("prow", "pcol")
    return jax.shard_map(shards, mesh=mesh, in_specs=in_specs, out_specs=out_specs, check_vma=False)
```

profile of v0, /device:TPU:0, one launch (start us, length us, event | category | flops | bytes accessed | tf_op | source)
XLA Modules:
  0.0 474.5 jit_solution(15905027569336554562)
XLA Ops:
  8.2 2.7 gather_fusion
  10.8 2.9 copy.50
  13.8 3.2 select_select_fusion.1
  17.0 2.9 copy.72
  21.8 3.1 broadcast_select_fusion.1
  25.0 39.0 %reduce-scatter.7.cloned.1.call-done = f32[64,1024]{1,0:T(8,128)} async-done(((f32[512,1024]{1,0:T(8,128)}), f32[64,1024]{1,0:T(8,128)}) %reduce-scatter.7.cloned.1.call-update) | async-done | bytes 262160 | tf_op jit(solution)/shard_map/reduce_scatter | solution.py:48
  65.9 63.2 %all-reduce.5.cloned.1.call-done = f32[512,1024]{0,1:T(8,128)} async-done(((f32[512,1024]{0,1:T(8,128)}), f32[512,1024]{0,1:T(8,128)}) %all-reduce.5.cloned.1.call-update) | async-done | bytes 2097168 | tf_op jit(solution)/shard_map/psum | solution.py:9
  129.0 2.9 copy.54
  131.9 19.5 %scatter_custom_fusion = f32[512,1024]{1,0:T(8,128)S(1)} fusion(f32[512,1024]{1,0:T(8,128)S(1)} %copy.85, s32[512]{0:T(512)S(1)} %bitcast.75, f32[]{:T(128)} %constant.160.clone.4, pred[512]{0:T(512)(128)(4,1)S(1)} %compare_and_fusion.2, f32[512,1024]{1,0:T(8,128)} %copy.54, s32[1024]{0:T(1024)S(1)} %pad_clamp_fusion.2), kind=kCustom, calls=%fused_computation.17 | custom fusion | flops 524288 | bytes 4198916 | tf_op jit(solution)/shard_map/scatter | solution.py:60
  153.2 5.0 %all-gather.3.cloned.1.call-done = f32[512,1024]{1,0:T(8,128)} async-done(((f32[64,1024]{1,0:T(8,128)}), f32[512,1024]{1,0:T(8,128)}) %all-gather.3.cloned.1.call-update) | async-done | bytes 2097168 | tf_op jit(solution)/shard_map/all_gather | solution.py:49
  158.2 2.9 copy.52
  161.1 10.8 %fusion.2 = (f32[512,1024]{0,1:T(8,128)S(1)}, f32[1024,512]{1,0:T(8,128)}) fusion(f32[512,1024]{0,1:T(8,128)} %copy.55, f32[512,1024]{0,1:T(8,128)} %copy.52, pred[1024]{0:T(1024)(128)(4,1)S(1)} %fusion.41, pred[]{:T(512)S(6)} %eq.31, f32[512,1024]{1,0:T(8,128)} %all-gather.3.cloned.1.call-done, f32[2,512,512]{2,1,0:T(8,128)} %param.20), kind=kOutput, calls=%fused_computation.12 | convolution fusion | flops 3222274048 | bytes 11535361 | tf_op jit(solution)/shard_map/dot_general | solution.py:29
  171.9 2.9 convolution_select_fusion.1
  175.7 51.7 %all-reduce.7.cloned.1.call-done = f32[512,512]{0,1:T(8,128)} async-done(((f32[512,512]{0,1:T(8,128)}), f32[512,512]{0,1:T(8,128)}) %all-reduce.7.cloned.1.call-update) | async-done | bytes 1048592 | tf_op jit(solution)/shard_map/psum | solution.py:9
  227.4 6.9 %fusion.8 = f32[512,1024]{0,1:T(8,128)} fusion(f32[512,1024]{0,1:T(8,128)S(1)} %get-tuple-element.86, f32[1024,512]{1,0:T(8,128)} %get-tuple-element.87, f32[512,512]{0,1:T(8,128)} %all-reduce.7.cloned.1.call-done, pred[1024]{0:T(1024)(128)(4,1)S(1)} %fusion.41, pred[512]{0:T(512)(128)(4,1)S(1)} %fusion.44), kind=kOutput, calls=%fused_computation.20 | convolution fusion | flops 3222536192 | bytes 7341568 | tf_op jit(solution)/shard_map/dot_general | solution.py:29
  234.3 3.0 fusion.10
  239.2 2.7 gather_fusion.1
  241.9 2.9 copy.59
  244.8 3.2 select_select_fusion
  248.0 2.9 copy.74
  252.6 39.1 %reduce-scatter.9.cloned.1.call-done = f32[64,1024]{1,0:T(8,128)} async-done(((f32[512,1024]{1,0:T(8,128)}), f32[64,1024]{1,0:T(8,128)}) %reduce-scatter.9.cloned.1.call-update) | async-done | bytes 262160 | tf_op jit(solution)/shard_map/reduce_scatter | solution.py:48
  293.0 63.5 %all-reduce.9.cloned.1.call-done = f32[512,1024]{0,1:T(8,128)} async-done(((f32[512,1024]{0,1:T(8,128)}), f32[512,1024]{0,1:T(8,128)}) %all-reduce.9.cloned.1.call-update) | async-done | bytes 2097168 | tf_op jit(solution)/shard_map/psum | solution.py:9
  356.5 2.9 copy.62
  359.4 19.6 %scatter_custom_fusion.1 = f32[512,1024]{1,0:T(8,128)S(1)} fusion(f32[512,1024]{1,0:T(8,128)S(1)} %copy.58, s32[512]{0:T(512)S(1)} %bitcast.74, f32[]{:T(128)} %constant.160.clone.4, pred[512]{0:T(512)(128)(4,1)S(1)} %compare_and_fusion, f32[512,1024]{1,0:T(8,128)} %copy.62, s32[1024]{0:T(1024)S(1)} %pad_clamp_fusion), kind=kCustom, calls=%fused_computation.14 | custom fusion | flops 524288 | bytes 4198916 | tf_op jit(solution)/shard_map/scatter | solution.py:60
  380.8 4.9 %all-gather.5.cloned.1.call-done = f32[512,1024]{1,0:T(8,128)} async-done(((f32[64,1024]{1,0:T(8,128)}), f32[512,1024]{1,0:T(8,128)}) %all-gather.5.cloned.1.call-update) | async-done | bytes 2097168 | tf_op jit(solution)/shard_map/all_gather | solution.py:49
  385.7 3.1 copy.61
  388.8 11.4 %fusion = (f32[512,1024]{0,1:T(8,128)S(1)}, f32[1024,512]{1,0:T(8,128)}) fusion(f32[512,1024]{0,1:T(8,128)} %copy.64, f32[512,1024]{0,1:T(8,128)} %copy.61, pred[1024]{0:T(1024)(128)(4,1)S(1)} %fusion.42, pred[]{:T(512)S(6)} %eq.30, f32[512,1024]{1,0:T(8,128)} %all-gather.5.cloned.1.call-done, f32[2,512,512]{2,1,0:T(8,128)} %param.20), kind=kOutput, calls=%fused_computation.8 | convolution fusion | flops 3222274048 | bytes 11535361 | tf_op jit(solution)/shard_map/dot_general | solution.py:29
  400.3 2.9 convolution_select_fusion
  403.2 51.9 %all-reduce.11.cloned.1.call-done = f32[512,512]{0,1:T(8,128)} async-done(((f32[512,512]{0,1:T(8,128)}), f32[512,512]{0,1:T(8,128)}) %all-reduce.11.cloned.1.call-update) | async-done | bytes 1048592 | tf_op jit(solution)/shard_map/psum | solution.py:9
  455.2 6.9 %fusion.9 = f32[512,1024]{0,1:T(8,128)} fusion(f32[512,1024]{0,1:T(8,128)S(1)} %get-tuple-element.88, f32[1024,512]{1,0:T(8,128)} %get-tuple-element.89, f32[512,512]{0,1:T(8,128)} %all-reduce.11.cloned.1.call-done, pred[1024]{0:T(1024)(128)(4,1)S(1)} %fusion.42, pred[512]{0:T(512)(128)(4,1)S(1)} %fusion.43), kind=kOutput, calls=%fused_computation.21 | convolution fusion | flops 3222536192 | bytes 7341568 | tf_op jit(solution)/shard_map/dot_general | solution.py:29
  462.1 2.5 fusion.11
  464.5 2.9 copy.67
  (70 shorter events, 14.9 us)
Async XLA Ops:
  6.5 1.6 copy-start.4
  6.5 57.4 %reduce-scatter.7.cloned.1.call-start = ((), (), s32[]{:S(2)}) async-start(), calls=%async_computation.8 | async-start | bytes 2359296 | tf_op jit(solution)/shard_map/reduce_scatter | solution.py:48
  19.9 109.1 %all-reduce.5.cloned.1.call-start = ((), (), s32[]{:S(2)}) async-start(), calls=%async_computation.3 | async-start | bytes 4194304 | tf_op jit(solution)/shard_map/psum | solution.py:9
  25.0 133.2 %all-gather.3.cloned.1.call-start = ((), (), s32[]{:S(2)}) async-start(), calls=%async_computation.2 | async-start | bytes 2359296 | tf_op jit(solution)/shard_map/all_gather | solution.py:49
  64.0 163.4 %all-reduce.7.cloned.1.call-start = ((), (), s32[]{:S(2)}) async-start(), calls=%async_computation.4 | async-start | bytes 2097152 | tf_op jit(solution)/shard_map/psum | solution.py:9
  161.1 10.8 %copy-start.2 = (f32[2,512,512]{2,1,0:T(8,128)S(1)}, f32[2,512,512]{2,1,0:T(8,128)}, u32[]{:S(2)}) copy-start(f32[2,512,512]{2,1,0:T(8,128)} %param.21) | copy-start | bytes 6291460
  174.8 116.8 %reduce-scatter.9.cloned.1.call-start = ((), (), s32[]{:S(2)}) async-start(), calls=%async_computation.9 | async-start | bytes 2359296 | tf_op jit(solution)/shard_map/reduce_scatter | solution.py:48
  227.4 6.9 %copy-start = (f32[512,512]{0,1:T(8,128)S(1)}, f32[512,512]{0,1:T(8,128)}, u32[]{:S(2)}) copy-start(f32[512,512]{0,1:T(8,128)} %all-reduce.7.cloned.1.call-done) | copy-start | bytes 3145732
  250.9 105.7 %all-reduce.9.cloned.1.call-start = ((), (), s32[]{:S(2)}) async-start(), calls=%async_computation.6 | async-start | bytes 4194304 | tf_op jit(solution)/shard_map/psum | solution.py:9
  252.5 133.2 %all-gather.5.cloned.1.call-start = ((), (), s32[]{:S(2)}) async-start(), calls=%async_computation.5 | async-start | bytes 2359296 | tf_op jit(solution)/shard_map/all_gather | solution.py:49
  291.7 163.5 %all-reduce.11.cloned.1.call-start = ((), (), s32[]{:S(2)}) async-start(), calls=%async_computation.7 | async-start | bytes 2097152 | tf_op jit(solution)/shard_map/psum | solution.py:9
  388.8 11.4 %copy-start.3 = (f32[2,512,512]{2,1,0:T(8,128)S(1)}, f32[2,512,512]{2,1,0:T(8,128)}, u32[]{:S(2)}) copy-start(f32[2,512,512]{2,1,0:T(8,128)} %param.21) | copy-start | bytes 6291460
  455.2 6.9 %copy-start.1 = (f32[512,512]{0,1:T(8,128)S(1)}, f32[512,512]{0,1:T(8,128)}, u32[]{:S(2)}) copy-start(f32[512,512]{0,1:T(8,128)} %all-reduce.11.cloned.1.call-done) | copy-start | bytes 3145732
Sparse Core Ops, SparseCore 0:
  20.0 43.8 reduce-scatter.6
  67.5 61.4 all-reduce.4
  131.1 27.0 all-gather.2
  175.0 52.4 all-reduce.6
  251.0 40.5 reduce-scatter.8
  295.1 61.4 all-reduce.8
  358.6 27.0 all-gather.4
  403.3 51.8 all-reduce.10
where the time goes:
time: 482 us; the launch traced here: 474 us
  waiting for transfers between devices  318 us (66%)
  other arithmetic  59 us (12%)
  matrix products  41.9 us (9%)
  local copies, waits for them, and re-layouts  41 us (9%)
  between operations  13.9 us (3%)
    psum x4, waiting for transfers between devices, broadcast(): return lax.psum(block, axis)  230 us
    reduce_scatter x2, waiting for transfers between devices, shards(): reduced = lax.psum_scatter(picked, 'prow', scatter_dimension=0, tiled=True)  78 us
    dot_general x6, matrix products, product(): jnp.dot(left, right, precision=lax.Precision.HIGHEST, preferred_element_t...  41.9 us
    scatter x2, other arithmetic, shards(): swapped = current.at[dest_local].set(moved, mode='drop')  39.1 us
    gather x4, local copies, waits for them, and re-layouts, shards(): jnp.take(current, jnp.clip(offset, 0, local_rows - 1), axis=0)  11.1 us
    all_gather x2, waiting for transfers between devices, shards(): raw_top = lax.all_gather(reduced, 'prow', axis=0, tiled=True)  9.83 us
  transfers between devices with their start and end apart: 8, of which 8 were waited for; matrix products, arithmetic and copies ran while one was open for 12% of the time, Pallas kernels for 0%

commit v1 on v0

--- a/solution.py
+++ b/solution.py
@@ -2,6 +2,27 @@
 import jax.numpy as jnp
 from jax import lax
 from jax.sharding import PartitionSpec as P
+
+
+def collect(x, axis, dim):
+    devices, index, extent = (lax.axis_size(axis), lax.axis_index(axis), x.shape[dim])
+    right = [(i, (i + 1) % devices) for i in range(devices)]
+    backward = [(i, (i - 1) % devices) for i in range(devices)]
+    result = jnp.zeros((*x.shape[:dim], devices * extent, *x.shape[dim + 1 :]), x.dtype)
+    result = lax.dynamic_update_slice_in_dim(result, x, index * extent, axis=dim)
+    from_left = from_right = x
+    middle = devices // 2
+    for step in range(1, middle + 1):
+        from_left = lax.ppermute(from_left, axis, right)
+        result = lax.dynamic_update_slice_in_dim(
+            result, from_left, (index - step) % devices * extent, axis=dim
+        )
+        if step < devices - middle:
+            from_right = lax.ppermute(from_right, axis, backward)
+            result = lax.dynamic_update_slice_in_dim(
+                result, from_right, (index + step) % devices * extent, axis=dim
+            )
+    return result
 
 
 def broadcast(block, axis, holder):
@@ -46,7 +67,7 @@
         picked = jnp.where(owned_rows[:, None], gathered_rows, 0.0)
         beyond = col_ids >= end_row
         reduced = lax.psum_scatter(picked, "prow", scatter_dimension=0, tiled=True)
-        raw_top = lax.all_gather(reduced, "prow", axis=0, tiled=True)
+        raw_top = collect(reduced, "prow", 0)
         solved = product(lower_inv[panel_index], raw_top)
         top_block = jnp.where(beyond[None, :], solved, raw_top)
         top_masked = jnp.where(beyond[None, :], solved, 0.0)

time: 482 us -> 543 us (1.13)
  local copies, waits for them, and re-layouts: 41 us -> 99.6 us
  starting transfers between devices: 0.46 us -> 17.3 us
  waiting for transfers between devices: 318 us -> 308 us
  matrix products: 41.9 us -> 35.3 us
    unnamed x8, waiting for transfers between devices: 0.13 us -> 78.3 us
    reduce_scatter x2 -> x0, waiting for transfers between devices: 78 us -> none  [shards(): reduced = lax.psum_scatter(picked, 'prow', scatter_dimension=0, tiled=True)]
    psum x4, waiting for transfers between devices: 230 us -> 152 us  [broadcast(): return lax.psum(block, axis)]
    ppermute x0 -> x14, waiting for transfers between devices: none -> 77.1 us  [the longest x8 50.9 us: collect(): from_left = lax.ppermute(from_left, axis, right)]
    dynamic_update_slice x0 -> x16, local copies, waits for them, and re-layouts: none -> 59.2 us  [the longest x8 28.4 us: collect(): lax.dynamic_update_slice_in_dim(result, from_left, (index - step) % devic...]
    ppermute x0 -> x14, starting transfers between devices: none -> 16.9 us  [the longest x6 16.8 us: collect(): from_right = lax.ppermute(from_right, axis, backward)]
    all_gather x2 -> x0, waiting for transfers between devices: 9.83 us -> none  [shards(): raw_top = lax.all_gather(reduced, 'prow', axis=0, tiled=True)]
    dot_general x6, matrix products: 41.9 us -> 35.3 us  [product(): jnp.dot(left, right, precision=lax.Precision.HIGHEST, preferred_element_t...]
  transfers between devices with their start and end apart: 8 -> 20, of which waited for: 8 -> 16; matrix products, arithmetic and copies ran while one was open for 12% -> 22% of each run, Pallas kernels for 0% -> 0%
where the time goes in v1:
time: 543 us; the launch traced here: 534 us
  waiting for transfers between devices  308 us (57%)
  local copies, waits for them, and re-layouts  99.6 us (18%)
  other arithmetic  59.2 us (11%)
  matrix products  35.3 us (7%)
  starting transfers between devices  17.3 us (3%)
  between operations  14.3 us (3%)
    psum x4, waiting for transfers between devices, broadcast(): return lax.psum(block, axis)  152 us
    unnamed x8, waiting for transfers between devices  78.3 us
    ppermute x8, waiting for transfers between devices, collect(): from_left = lax.ppermute(from_left, axis, right)  50.9 us
    scatter x2, other arithmetic, shards(): swapped = current.at[dest_local].set(moved, mode='drop')  39.3 us
    dot_general x6, matrix products, product(): jnp.dot(left, right, precision=lax.Precision.HIGHEST, preferred_element_t...  35.3 us
    dynamic_update_slice x8, local copies, waits for them, and re-layouts, collect(): lax.dynamic_update_slice_in_dim(result, from_left, (index - step) % devic...  28.4 us
    ppermute x6, waiting for transfers between devices, collect(): from_right = lax.ppermute(from_right, axis, backward)  26.2 us
    dynamic_update_slice x6, local copies, waits for them, and re-layouts, collect(): lax.dynamic_update_slice_in_dim(result, from_right, (index + step) % devi...  23.6 us
  transfers between devices with their start and end apart: 20, of which 16 were waited for; matrix products, arithmetic and copies ran while one was open for 22% of the time, Pallas kernels for 0%

profile of v1, /device:TPU:0, one launch (start us, length us, event | category | flops | bytes accessed | tf_op | source)
XLA Modules:
  0.0 533.6 jit_solution(17120316970074713340)
XLA Ops:
  25.8 38.2 %reduce-scatter.7.cloned.1.call-done = f32[64,1024]{1,0:T(8,128)} async-done(((f32[512,1024]{1,0:T(8,128)}), f32[64,1024]{1,0:T(8,128)}) %reduce-scatter.7.cloned.1.call-update) | async-done | bytes 262160
  68.4 13.2 %collective-permute-done = f32[64,1024]{0,1:T(8,128)S(1)} collective-permute-done((f32[64,1024]{0,1:T(8,128)S(1)}, f32[64,1024]{0,1:T(8,128)S(1)}, u32[]{:S(2)}, u32[]{:S(2)}) %collective-permute-start) | collective-permute-done | bytes 262176 | tf_op jit(solution)/shard_map/ppermute | solution.py:16
  81.9 5.5 %collective-permute-done.1 = f32[64,1024]{0,1:T(8,128)} collective-permute-done((f32[64,1024]{0,1:T(8,128)S(1)}, f32[64,1024]{0,1:T(8,128)}, u32[]{:S(2)}, u32[]{:S(2)}) %collective-permute-start.1) | collective-permute-done | bytes 262176 | tf_op jit(solution)/shard_map/ppermute | solution.py:21
  90.3 8.3 %collective-permute-done.2 = f32[64,1024]{0,1:T(8,128)} collective-permute-done((f32[64,1024]{0,1:T(8,128)S(1)}, f32[64,1024]{0,1:T(8,128)}, u32[]{:S(2)}, u32[]{:S(2)}) %collective-permute-start.2) | collective-permute-done | bytes 262176 | tf_op jit(solution)/shard_map/ppermute | solution.py:16
  98.6 3.8 collective-permute-done.3
  105.2 8.1 %collective-permute-done.4 = f32[64,1024]{0,1:T(8,128)} collective-permute-done((f32[64,1024]{0,1:T(8,128)}, f32[64,1024]{0,1:T(8,128)}, u32[]{:S(2)}, u32[]{:S(2)}) %collective-permute-start.4) | collective-permute-done | bytes 262176 | tf_op jit(solution)/shard_map/ppermute | solution.py:16
  113.5 25.3 %all-reduce.5.cloned.1.call-done = f32[512,1024]{0,1:T(8,128)} async-done(((f32[512,1024]{0,1:T(8,128)}), f32[512,1024]{0,1:T(8,128)}) %all-reduce.5.cloned.1.call-update) | async-done | bytes 2097168 | tf_op jit(solution)/shard_map/psum | solution.py:30
  141.7 19.5 %scatter_custom_fusion = f32[512,1024]{1,0:T(8,128)S(1)} fusion(f32[512,1024]{1,0:T(8,128)S(1)} %copy.93, s32[512]{0:T(512)S(1)} %bitcast.75, f32[]{:T(128)} %constant.216.clone.4, pred[512]{0:T(512)(128)(4,1)S(1)} %compare_and_fusion.2, f32[512,1024]{1,0:T(8,128)} %copy.48, s32[1024]{0:T(1024)S(1)} %pad_clamp_fusion.2), kind=kCustom, calls=%fused_computation.17 | custom fusion | flops 524288 | bytes 4198916 | tf_op jit(solution)/shard_map/scatter | solution.py:81
  171.5 4.1 dynamic_update_slice.50
  178.7 3.7 dynamic_update_slice.52
  182.4 4.1 dynamic_update_slice.53
  186.5 4.1 dynamic_update_slice.54
  190.6 3.7 dynamic_update_slice.55
  194.3 7.5 %fusion.2 = (f32[512,1024]{0,1:T(8,128)S(1)}, f32[1024,512]{1,0:T(8,128)}) fusion(f32[512,1024]{0,1:T(8,128)} %copy.49, f32[512,1024]{0,1:T(8,128)} %dynamic_update_slice.55, pred[1024]{0:T(1024)(128)(4,1)S(1)} %fusion.41, pred[]{:T(512)S(6)} %eq.82, f32[2,512,512]{2,1,0:T(8,128)} %param.20), kind=kOutput, calls=%fused_computation.12 | convolution fusion | flops 3222274048 | bytes 11535361 | tf_op jit(solution)/shard_map/dot_general | solution.py:50
  205.7 50.9 %all-reduce.7.cloned.1.call-done = f32[512,512]{0,1:T(8,128)} async-done(((f32[512,512]{0,1:T(8,128)}), f32[512,512]{0,1:T(8,128)}) %all-reduce.7.cloned.1.call-update) | async-done | bytes 1048592 | tf_op jit(solution)/shard_map/psum | solution.py:30
  256.6 6.9 %fusion.8 = f32[512,1024]{0,1:T(8,128)} fusion(f32[512,1024]{0,1:T(8,128)S(1)} %get-tuple-element.86, f32[1024,512]{1,0:T(8,128)} %get-tuple-element.87, f32[512,512]{0,1:T(8,128)} %all-reduce.7.cloned.1.call-done, pred[1024]{0:T(1024)(128)(4,1)S(1)} %fusion.41, pred[512]{0:T(512)(128)(4,1)S(1)} %get-tuple-element.90), kind=kOutput, calls=%fused_computation.20 | convolution fusion | flops 3222536192 | bytes 7341568 | tf_op jit(solution)/shard_map/dot_general | solution.py:50
  280.8 40.0 %reduce-scatter.9.cloned.1.call-done = f32[64,1024]{1,0:T(8,128)} async-done(((f32[512,1024]{1,0:T(8,128)}), f32[64,1024]{1,0:T(8,128)}) %reduce-scatter.9.cloned.1.call-update) | async-done | bytes 262160
  326.4 8.3 %collective-permute-done.7 = f32[64,1024]{0,1:T(8,128)S(1)} collective-permute-done((f32[64,1024]{0,1:T(8,128)S(1)}, f32[64,1024]{0,1:T(8,128)S(1)}, u32[]{:S(2)}, u32[]{:S(2)}) %collective-permute-start.7) | collective-permute-done | bytes 262176 | tf_op jit(solution)/shard_map/ppermute | solution.py:16
  335.2 10.4 %collective-permute-done.8 = f32[64,1024]{0,1:T(8,128)S(1)} collective-permute-done((f32[64,1024]{0,1:T(8,128)S(1)}, f32[64,1024]{0,1:T(8,128)S(1)}, u32[]{:S(2)}, u32[]{:S(2)}) %collective-permute-start.8) | collective-permute-done | bytes 262176 | tf_op jit(solution)/shard_map/ppermute | solution.py:21
  348.4 5.8 %collective-permute-done.9 = f32[64,1024]{0,1:T(8,128)S(1)} collective-permute-done((f32[64,1024]{0,1:T(8,128)S(1)}, f32[64,1024]{0,1:T(8,128)S(1)}, u32[]{:S(2)}, u32[]{:S(2)}) %collective-permute-start.9) | collective-permute-done | bytes 262176 | tf_op jit(solution)/shard_map/ppermute | solution.py:16
  354.3 6.5 %collective-permute-done.10 = f32[64,1024]{0,1:T(8,128)} collective-permute-done((f32[64,1024]{0,1:T(8,128)S(1)}, f32[64,1024]{0,1:T(8,128)}, u32[]{:S(2)}, u32[]{:S(2)}) %collective-permute-start.10) | collective-permute-done | bytes 262176 | tf_op jit(solution)/shard_map/ppermute | solution.py:21
  363.7 7.3 %collective-permute-done.11 = f32[64,1024]{0,1:T(8,128)} collective-permute-done((f32[64,1024]{0,1:T(8,128)S(1)}, f32[64,1024]{0,1:T(8,128)}, u32[]{:S(2)}, u32[]{:S(2)}) %collective-permute-start.11) | collective-permute-done | bytes 262176 | tf_op jit(solution)/shard_map/ppermute | solution.py:16
  371.0 25.0 %all-reduce.9.cloned.1.call-done = f32[512,1024]{0,1:T(8,128)} async-done(((f32[512,1024]{0,1:T(8,128)}), f32[512,1024]{0,1:T(8,128)}) %all-reduce.9.cloned.1.call-update) | async-done | bytes 2097168 | tf_op jit(solution)/shard_map/psum | solution.py:30
  398.9 19.8 %scatter_custom_fusion.1 = f32[512,1024]{1,0:T(8,128)S(1)} fusion(f32[512,1024]{1,0:T(8,128)S(1)} %copy.52, s32[512]{0:T(512)S(1)} %bitcast.74, f32[]{:T(128)} %constant.216.clone.4, pred[512]{0:T(512)(128)(4,1)S(1)} %compare_and_fusion, f32[512,1024]{1,0:T(8,128)} %copy.54, s32[1024]{0:T(1024)S(1)} %pad_clamp_fusion), kind=kCustom, calls=%fused_computation.14 | custom fusion | flops 524288 | bytes 4198916 | tf_op jit(solution)/shard_map/scatter | solution.py:81
  429.1 4.0 dynamic_update_slice.58
  435.9 3.7 dynamic_update_slice.60
  439.6 4.1 dynamic_update_slice.61
  443.7 4.1 dynamic_update_slice.62
  447.8 4.0 dynamic_update_slice.63
  451.8 8.2 %fusion = (f32[512,1024]{0,1:T(8,128)S(1)}, f32[1024,512]{1,0:T(8,128)}) fusion(f32[512,1024]{0,1:T(8,128)} %copy.56, f32[512,1024]{0,1:T(8,128)} %dynamic_update_slice.63, pred[1024]{0:T(1024)(128)(4,1)S(1)} %fusion.42, pred[]{:T(512)S(6)} %eq.81, f32[2,512,512]{2,1,0:T(8,128)} %param.20), kind=kOutput, calls=%fused_computation.8 | convolution fusion | flops 3222274048 | bytes 11535361 | tf_op jit(solution)/shard_map/dot_general | solution.py:50
  462.9 51.1 %all-reduce.11.cloned.1.call-done = f32[512,512]{0,1:T(8,128)} async-done(((f32[512,512]{0,1:T(8,128)}), f32[512,512]{0,1:T(8,128)}) %all-reduce.11.cloned.1.call-update) | async-done | bytes 1048592 | tf_op jit(solution)/shard_map/psum | solution.py:30
  514.1 6.9 %fusion.9 = f32[512,1024]{0,1:T(8,128)} fusion(f32[512,1024]{0,1:T(8,128)S(1)} %get-tuple-element.88, f32[1024,512]{1,0:T(8,128)} %get-tuple-element.89, f32[512,512]{0,1:T(8,128)} %all-reduce.11.cloned.1.call-done, pred[1024]{0:T(1024)(128)(4,1)S(1)} %fusion.42, pred[512]{0:T(512)(128)(4,1)S(1)} %fusion.43), kind=kOutput, calls=%fused_computation.21 | convolution fusion | flops 3222536192 | bytes 7341568 | tf_op jit(solution)/shard_map/dot_general | solution.py:50
  (117 shorter events, 103.2 us)
Async XLA Ops:
  6.5 1.6 copy-start.8
  6.5 57.4 %reduce-scatter.7.cloned.1.call-start = ((), (), s32[]{:S(2)}) async-start(), calls=%async_computation.6 | async-start | bytes 2359296
  19.9 118.9 %all-reduce.5.cloned.1.call-start = ((), (), s32[]{:S(2)}) async-start(), calls=%async_computation.2 | async-start | bytes 4194304 | tf_op jit(solution)/shard_map/psum | solution.py:30
  24.9 231.7 %all-reduce.7.cloned.1.call-start = ((), (), s32[]{:S(2)}) async-start(), calls=%async_computation.3 | async-start | bytes 2097152 | tf_op jit(solution)/shard_map/psum | solution.py:30
  65.1 16.4 %collective-permute-start = (f32[64,1024]{0,1:T(8,128)S(1)}, f32[64,1024]{0,1:T(8,128)S(1)}, u32[]{:S(2)}, u32[]{:S(2)}) collective-permute-start(f32[64,1024]{0,1:T(8,128)S(1)} %copy.65), channel_id=1, source_target_pairs={{0,4},{4,8},{8,12},{12,16},{16,20},{20,24},{24,28},{28,0},{1,5},{5... | collective-permute-start | bytes 786440 | tf_op jit(solution)/shard_map/ppermute | solution.py:16
  65.7 21.7 %collective-permute-start.1 = (f32[64,1024]{0,1:T(8,128)S(1)}, f32[64,1024]{0,1:T(8,128)}, u32[]{:S(2)}, u32[]{:S(2)}) collective-permute-start(f32[64,1024]{0,1:T(8,128)S(1)} %copy.65), channel_id=1, source_target_pairs={{0,28},{4,0},{8,4},{12,8},{16,12},{20,16},{24,20},{28,24},{1,29},{... | collective-permute-start | bytes 786440 | tf_op jit(solution)/shard_map/ppermute | solution.py:21
  81.5 17.1 %collective-permute-start.2 = (f32[64,1024]{0,1:T(8,128)S(1)}, f32[64,1024]{0,1:T(8,128)}, u32[]{:S(2)}, u32[]{:S(2)}) collective-permute-start(f32[64,1024]{0,1:T(8,128)S(1)} %collective-permute-done), channel_id=1, source_target_pairs={{0,4},{4,8},{8,12},{12,16},{16,20},{20,24},{24,28},{28,0},{1,5},{5... | collective-permute-start | bytes 786440 | tf_op jit(solution)/shard_map/ppermute | solution.py:16
  87.4 15.0 %collective-permute-start.3 = (f32[64,1024]{0,1:T(8,128)}, f32[64,1024]{0,1:T(8,128)}, u32[]{:S(2)}, u32[]{:S(2)}) collective-permute-start(f32[64,1024]{0,1:T(8,128)} %collective-permute-done.1), channel_id=1, source_target_pairs={{0,28},{4,0},{8,4},{12,8},{16,12},{20,16},{24,20},{28,24},{1,29},{... | collective-permute-start | bytes 786440 | tf_op jit(solution)/shard_map/ppermute | solution.py:21
  98.6 14.7 %collective-permute-start.4 = (f32[64,1024]{0,1:T(8,128)}, f32[64,1024]{0,1:T(8,128)}, u32[]{:S(2)}, u32[]{:S(2)}) collective-permute-start(f32[64,1024]{0,1:T(8,128)} %collective-permute-done.2), channel_id=1, source_target_pairs={{0,4},{4,8},{8,12},{12,16},{16,20},{20,24},{24,28},{28,0},{1,5},{5... | collective-permute-start | bytes 786440 | tf_op jit(solution)/shard_map/ppermute | solution.py:16
  102.4 84.1 %collective-permute-start.5 = (f32[64,1024]{0,1:T(8,128)}, f32[64,1024]{0,1:T(8,128)}, u32[]{:S(2)}, u32[]{:S(2)}) collective-permute-start(f32[64,1024]{0,1:T(8,128)} %collective-permute-done.3), channel_id=1, source_target_pairs={{0,28},{4,0},{8,4},{12,8},{16,12},{20,16},{24,20},{28,24},{1,29},{... | collective-permute-start | bytes 786440 | tf_op jit(solution)/shard_map/ppermute | solution.py:21
  113.3 77.3 %collective-permute-start.6 = (f32[64,1024]{0,1:T(8,128)}, f32[64,1024]{0,1:T(8,128)}, u32[]{:S(2)}, u32[]{:S(2)}) collective-permute-start(f32[64,1024]{0,1:T(8,128)} %collective-permute-done.4), channel_id=1, source_target_pairs={{0,4},{4,8},{8,12},{12,16},{16,20},{20,24},{24,28},{28,0},{1,5},{5... | collective-permute-start | bytes 786440 | tf_op jit(solution)/shard_map/ppermute | solution.py:16
  194.3 7.6 %copy-start.2 = (f32[2,512,512]{2,1,0:T(8,128)S(1)}, f32[2,512,512]{2,1,0:T(8,128)}, u32[]{:S(2)}) copy-start(f32[2,512,512]{2,1,0:T(8,128)} %param.21) | copy-start | bytes 6291460
  204.8 116.0 %reduce-scatter.9.cloned.1.call-start = ((), (), s32[]{:S(2)}) async-start(), calls=%async_computation.7 | async-start | bytes 2359296
  256.6 6.9 %copy-start = (f32[512,512]{0,1:T(8,128)S(1)}, f32[512,512]{0,1:T(8,128)}, u32[]{:S(2)}) copy-start(f32[512,512]{0,1:T(8,128)} %all-reduce.7.cloned.1.call-done) | copy-start | bytes 3145732
  280.0 116.0 %all-reduce.9.cloned.1.call-start = ((), (), s32[]{:S(2)}) async-start(), calls=%async_computation.4 | async-start | bytes 4194304 | tf_op jit(solution)/shard_map/psum | solution.py:30
  321.9 12.8 %collective-permute-start.7 = (f32[64,1024]{0,1:T(8,128)S(1)}, f32[64,1024]{0,1:T(8,128)S(1)}, u32[]{:S(2)}, u32[]{:S(2)}) collective-permute-start(f32[64,1024]{0,1:T(8,128)S(1)} %copy.67), channel_id=1, source_target_pairs={{0,4},{4,8},{8,12},{12,16},{16,20},{20,24},{24,28},{28,0},{1,5},{5... | collective-permute-start | bytes 786440 | tf_op jit(solution)/shard_map/ppermute | solution.py:16
  323.6 190.5 %all-reduce.11.cloned.1.call-start = ((), (), s32[]{:S(2)}) async-start(), calls=%async_computation.5 | async-start | bytes 2097152 | tf_op jit(solution)/shard_map/psum | solution.py:30
  323.8 21.9 %collective-permute-start.8 = (f32[64,1024]{0,1:T(8,128)S(1)}, f32[64,1024]{0,1:T(8,128)S(1)}, u32[]{:S(2)}, u32[]{:S(2)}) collective-permute-start(f32[64,1024]{0,1:T(8,128)S(1)} %copy.67), channel_id=1, source_target_pairs={{0,28},{4,0},{8,4},{12,8},{16,12},{20,16},{24,20},{28,24},{1,29},{... | collective-permute-start | bytes 786440 | tf_op jit(solution)/shard_map/ppermute | solution.py:21
  334.8 19.5 %collective-permute-start.9 = (f32[64,1024]{0,1:T(8,128)S(1)}, f32[64,1024]{0,1:T(8,128)S(1)}, u32[]{:S(2)}, u32[]{:S(2)}) collective-permute-start(f32[64,1024]{0,1:T(8,128)S(1)} %collective-permute-done.7), channel_id=1, source_target_pairs={{0,4},{4,8},{8,12},{12,16},{16,20},{20,24},{24,28},{28,0},{1,5},{5... | collective-permute-start | bytes 786440 | tf_op jit(solution)/shard_map/ppermute | solution.py:16
  345.6 8.6 %copy-start.4 = (f32[64,1024]{0,1:T(8,128)}, f32[64,1024]{0,1:T(8,128)S(1)}, u32[]{:S(2)}) copy-start(f32[64,1024]{0,1:T(8,128)S(1)} %collective-permute-done.8) | copy-start | bytes 786436
  345.6 15.2 %collective-permute-start.10 = (f32[64,1024]{0,1:T(8,128)S(1)}, f32[64,1024]{0,1:T(8,128)}, u32[]{:S(2)}, u32[]{:S(2)}) collective-permute-start(f32[64,1024]{0,1:T(8,128)S(1)} %collective-permute-done.8), channel_id=1, source_target_pairs={{0,28},{4,0},{8,4},{12,8},{16,12},{20,16},{24,20},{28,24},{1,29},{... | collective-permute-start | bytes 786440 | tf_op jit(solution)/shard_map/ppermute | solution.py:21
  354.2 6.6 %copy-start.6 = (f32[64,1024]{0,1:T(8,128)}, f32[64,1024]{0,1:T(8,128)S(1)}, u32[]{:S(2)}) copy-start(f32[64,1024]{0,1:T(8,128)S(1)} %collective-permute-done.9) | copy-start | bytes 786436
  354.2 16.7 %collective-permute-start.11 = (f32[64,1024]{0,1:T(8,128)S(1)}, f32[64,1024]{0,1:T(8,128)}, u32[]{:S(2)}, u32[]{:S(2)}) collective-permute-start(f32[64,1024]{0,1:T(8,128)S(1)} %collective-permute-done.9), channel_id=1, source_target_pairs={{0,4},{4,8},{8,12},{12,16},{16,20},{20,24},{24,28},{28,0},{1,5},{5... | collective-permute-start | bytes 786440 | tf_op jit(solution)/shard_map/ppermute | solution.py:16
  360.8 82.9 %collective-permute-start.12 = (f32[64,1024]{0,1:T(8,128)}, f32[64,1024]{0,1:T(8,128)}, u32[]{:S(2)}, u32[]{:S(2)}) collective-permute-start(f32[64,1024]{0,1:T(8,128)} %collective-permute-done.10), channel_id=1, source_target_pairs={{0,28},{4,0},{8,4},{12,8},{16,12},{20,16},{24,20},{28,24},{1,29},{... | collective-permute-start | bytes 786440 | tf_op jit(solution)/shard_map/ppermute | solution.py:21
  371.0 76.8 %collective-permute-start.13 = (f32[64,1024]{0,1:T(8,128)}, f32[64,1024]{0,1:T(8,128)}, u32[]{:S(2)}, u32[]{:S(2)}) collective-permute-start(f32[64,1024]{0,1:T(8,128)} %collective-permute-done.11), channel_id=1, source_target_pairs={{0,4},{4,8},{8,12},{12,16},{16,20},{20,24},{24,28},{28,0},{1,5},{5... | collective-permute-start | bytes 786440 | tf_op jit(solution)/shard_map/ppermute | solution.py:16
  420.6 8.5 %copy-start.5 = (f32[64,1024]{0,1:T(8,128)S(1)}, f32[64,1024]{0,1:T(8,128)}, u32[]{:S(2)}) copy-start(f32[64,1024]{0,1:T(8,128)} %copy-done.4) | copy-start | bytes 786436
  422.2 10.9 %copy-start.7 = (f32[64,1024]{0,1:T(8,128)S(1)}, f32[64,1024]{0,1:T(8,128)}, u32[]{:S(2)}) copy-start(f32[64,1024]{0,1:T(8,128)} %copy-done.6) | copy-start | bytes 786436
  451.8 8.2 %copy-start.3 = (f32[2,512,512]{2,1,0:T(8,128)S(1)}, f32[2,512,512]{2,1,0:T(8,128)}, u32[]{:S(2)}) copy-start(f32[2,512,512]{2,1,0:T(8,128)} %param.21) | copy-start | bytes 6291460
  514.1 6.9 %copy-start.1 = (f32[512,512]{0,1:T(8,128)S(1)}, f32[512,512]{0,1:T(8,128)}, u32[]{:S(2)}) copy-start(f32[512,512]{0,1:T(8,128)} %all-reduce.11.cloned.1.call-done) | copy-start | bytes 3145732
Sparse Core Ops, SparseCore 0:
  20.0 43.8 reduce-scatter.6
  67.5 71.2 all-reduce.4
  204.9 51.6 all-reduce.6
  280.2 40.5 reduce-scatter.8
  324.2 71.7 all-reduce.8
  463.0 51.0 all-reduce.10
